TPU v7x, 32 devices: a whole 2x2x4 slice. The times are simulated.
32 devices in a mesh: seq: 8 (over z, y), batch: 4 (over x, core).
Axes of the slice: x: 2, y: 2, z: 4, core: 2. Of those that a mesh axis runs over, the one named last changes fastest.
Arguments:
- signal: bfloat16 [4, 1024, 8192], P('batch', 'seq'), may hold values from -6 to 6
- out_grad: bfloat16 [4, 1024, 8192], P('batch', 'seq'), may hold values from -6 to 6
- residues: float32 [8, 8192], replicated, may hold values from -0.3 to 0.3
- log_rates: float32 [8, 512], replicated, as said below
Outputs:
- mixed: bfloat16 [4, 1024, 8192], P('batch', 'seq')
- grad_signal: bfloat16 [4, 1024, 8192], P('batch', 'seq')
- grad_residues: float32 [8, 8192], replicated
- grad_rates: float32 [8, 512], replicated
Inputs may be any that keep to these rules, and one draw needn't show every extreme that they name: Each decay rate exp(log_rates) lies between 0.2 / 1024 and 1 / 30.
All inputs are finite; a program needn't handle non-finite values.
Results may differ from a plain program's by a relative error of at most 0.0012.
Values sent between devices are 32-bit elements; how exact they have to be, the bound alone decides.
A program may use at most 384 MiB of HBM per device.

v0:
```python
import jax
import jax.numpy as jnp
from jax import lax
from jax.sharding import PartitionSpec as P

M = 8
GROUP = 16


HIGHEST = lax.Precision.HIGHEST
HIGHER = lax.Precision.HIGH


def carried_in(shard, axis, combine, identity, reverse):
    peers, index = (lax.axis_size(axis), lax.axis_index(axis))
    everything = jax.tree.map(lambda part: lax.all_gather(part, axis), shard)
    start = jax.tree.map(
        lambda part, zero: jnp.broadcast_to(jnp.asarray(zero, part.dtype), part.shape),
        shard,
        identity,
    )

    def lap(k, before):
        at = peers - 1 - k if reverse else k
        reached = at > index if reverse else at < index
        new = combine(before, jax.tree.map(lambda part: part[at], everything))
        return jax.tree.map(lambda a, b: jnp.where(reached, a, b), new, before)

    return lax.fori_loop(0, peers, lap, start)


def depthwise(values, kernel, padding, precision):
    return lax.conv_general_dilated(
        values,
        kernel[:, None, :],
        (1,),
        [padding],
        dimension_numbers=("NWC", "WIO", "NWC"),
        feature_group_count=values.shape[2],
        precision=precision,
        preferred_element_type=jnp.float32,
    )


def local(signal, out_grad, residues, log_rates):
    batch_rows, length, channels = signal.shape
    groups = log_rates.shape[1]
    decay_rate = jnp.exp(log_rates)
    offsets = jnp.arange(length + 1, dtype=jnp.float32)
    powers = jnp.exp(-decay_rate[None] * offsets[:, None, None])
    res_group = residues.reshape(M, groups, GROUP)
    kernel = jnp.einsum("kmg,mgi->kgi", powers[:length], res_group, precision=HIGHEST).reshape(
        length, channels
    )
    inputs = signal.astype(jnp.float32)
    cotangent = out_grad.astype(jnp.float32)
    local_out = depthwise(inputs, kernel[::-1], (length - 1, 0), HIGHER)
    local_grad = depthwise(cotangent, kernel, (0, length - 1), HIGHER)
    weights = jnp.stack([powers[:length], offsets[:length, None, None] * powers[:length]])
    starts_table = jnp.stack([powers[:length], offsets[1:, None, None] * powers[1:]])
    input_group = inputs.reshape(batch_rows, length, groups, GROUP)
    grad_group = cotangent.reshape(batch_rows, length, groups, GROUP)
    end_states = jnp.einsum("jsmg,bsgi->jbmgi", weights[:, ::-1], input_group, precision=HIGHER)
    start_sums = jnp.einsum("jtmg,btgi->jbmgi", starts_table, grad_group, precision=HIGHER)
    local_state = end_states[0]
    local_moment = end_states[1]
    start_state = start_sums[0]
    weighted_start = start_sums[1]
    first_pole = powers[1][None, :, :, None]
    start_plain = first_pole * start_state
    empty_state = jnp.zeros_like(local_state)
    span = jnp.full((), float(length), jnp.float32)
    no_span = jnp.zeros((), jnp.float32)

    def join_forward(earlier, later):
        decay = jnp.exp(-decay_rate * later[0])[None, :, :, None]
        return (
            earlier[0] + later[0],
            decay * earlier[1] + later[1],
            decay * (earlier[2] + later[0] * earlier[1]) + later[2],
        )

    def join_backward(earlier, later):
        decay = jnp.exp(-decay_rate * later[0])[None, :, :, None]
        return (earlier[0] + later[0], decay * earlier[1] + later[1])

    forward_out = carried_in(
        (span, local_state, local_moment),
        "seq",
        join_forward,
        (no_span, empty_state, empty_state),
        False,
    )
    carry_state = forward_out[1]
    carry_moment = forward_out[2]
    backward_out = carried_in(
        (span, start_state), "seq", join_backward, (no_span, empty_state), True
    )
    adjoint = backward_out[1]
    out_extra = jnp.einsum(
        "tmg,bmgi->btgi", powers[1:], res_group[None] * carry_state, precision=HIGHEST
    ).reshape(batch_rows, length, channels)
    grad_extra = jnp.einsum(
        "tmg,bmgi->btgi", powers[1:][::-1], res_group[None] * adjoint, precision=HIGHEST
    ).reshape(batch_rows, length, channels)
    mixed = (local_out + out_extra).astype(jnp.bfloat16)
    grad_signal = (local_grad + grad_extra).astype(jnp.bfloat16)
    lag_values = jnp.swapaxes(out_grad, 0, 1).reshape(1, length, batch_rows * channels)
    lag_kernel = jnp.swapaxes(signal, 0, 1).reshape(length, batch_rows * channels)
    lagged = depthwise(lag_values, lag_kernel, (0, length - 1), None)
    lag_sums = jnp.sum(lagged.reshape(length, batch_rows, groups, GROUP), axis=1)
    lag_terms = jnp.einsum("jkmg,kgi->jmgi", weights, lag_sums, precision=HIGHEST)
    residue_part = lag_terms[0] + jnp.sum(carry_state * start_plain, axis=0)
    moment_part = lag_terms[1] + jnp.sum(
        carry_state * weighted_start + carry_moment * start_plain, axis=0
    )
    rate_part = -decay_rate * jnp.sum(res_group * moment_part, axis=2)
    norm_factor = 1.0 / (batch_rows * lax.axis_size("batch") * length * lax.axis_size("seq"))
    grad_residues, grad_rates = lax.psum(
        (residue_part.reshape(M, channels) * norm_factor, rate_part * norm_factor), ("seq", "batch")
    )
    return (mixed, grad_signal, grad_residues, grad_rates)


def solution(mesh):
    placed = (P("batch", "seq", None), P("batch", "seq", None), P(), P())
    return jax.shard_map(
        local,
        mesh=mesh,
        in_specs=placed,
        out_specs=(P("batch", "seq", None), P("batch", "seq", None), P(), P()),
        check_vma=False,
    )
```

profile of v0, /device:TPU:0, one launch (start us, length us, event | category | flops | bytes accessed | tf_op | source)
XLA Modules:
  0.0 763.9 jit_solution(8605537450636845793)
XLA Ops:
  11.4 3.8 pad_maximum_fusion
  15.2 7.2 rev.10
  25.7 4.6 fusion.16
  36.5 6.5 fusion.9
  47.7 3.7 slice.55
  55.4 11.2 %fusion.23 = f32[512,128,16]{1,2,0:T(8,128)} fusion(f32[8,512,16]{2,1,0:T(8,128)S(1)} %reshape.109, f32[129,8,512]{0,1,2:T(8,128)} %copy-done), kind=kOutput, calls=%fused_computation.31 | convolution fusion | flops 100663296 | bytes 6553600 | tf_op jit(solution)/shard_map/kmg,mgi->kgi/dot_general | solution.py:52
  68.6 24.8 %all-reduce = f32[8]{0:T(128)} all-reduce(f32[8]{0:T(128)S(1)} %dynamic-update-slice), channel_id=1, replica_groups=mesh['seq'=8,'batch'=4] {'seq'}, use_global_device_ids=true, to_apply=%add | all-reduce | flops 8 | bytes 64
  93.5 62.1 %fusion.7 = f32[1,128,8192]{2,0,1:T(1,128)} fusion(bf16[128,1,8192]{2,0,1:T(8,128)(2,1)} %bitcast.133, bf16[1,128,8192]{2,1,0:T(8,128)(2,1)} %param.9), kind=kOutput, calls=%fused_computation.16 | convolution fusion | flops 135266304 | bytes 8388608 | tf_op jit(solution)/shard_map/conv_general_dilated | solution.py:33
  155.5 9.7 %copy.129 = f32[1,128,8192]{1,2,0:T(8,128)} copy(f32[1,128,8192]{2,0,1:T(1,128)} %fusion.7) | data formatting | bytes 8388608 | tf_op jit(solution)/shard_map/conv_general_dilated | solution.py:33
  165.2 12.2 %fusion.5 = f32[512,16,2,8]{1,3,2,0:T(8,128)} fusion(f32[128,512,16,1]{0,2,3,1:T(8,128)} %bitcast.123, f32[2,128,8,512]{1,2,3,0:T(8,128)} %get-tuple-element.514), kind=kOutput, calls=%fused_computation.14 | convolution fusion | flops 201326592 | bytes 8912896 | tf_op jit(solution)/shard_map/jkmg,kgi->jmgi/dot_general | solution.py:112
  177.4 3.7 copy.131
  185.7 9.6 %copy.119 = f32[128,1,8192]{2,1,0:T(1,128)} copy(f32[128,1,8192]{0,2,1:T(8,128)} %bitcast.121) | data formatting | bytes 8388608 | tf_op jit(solution)/shard_map/broadcast_in_dim;reshape | solution.py:35
  195.4 5.6 copy.108
  201.0 32.7 %rev.9 = f32[128,8192]{1,0:T(8,128)} reverse(f32[128,8192]{1,0:T(8,128)} %copy.108), dimensions={0} | reverse | bytes 8388608 | tf_op jit(solution)/shard_map/rev | solution.py:57
  233.6 6.6 broadcast_in_dim.16
  240.2 22.8 %all-gather.4.cloned.1.call-done = f32[8,1,8,512,16]{4,2,0,3,1:T(8,128)} async-done(((f32[1,1,8,512,16]{4,2,0,3,1:T(8,128)}), f32[8,1,8,512,16]{4,2,0,3,1:T(8,128)}) %all-gather.4.cloned.1.call-update) | async-done | bytes 2097168 | tf_op jit(solution)/shard_map/all_gather | solution.py:16
  263.0 10.3 %copy.113 = f32[8,1,8,512,16]{3,4,2,1,0:T(8,128)S(1)} copy(f32[8,1,8,512,16]{4,2,0,3,1:T(8,128)} %all-gather.4.cloned.1.call-done) | data formatting | bytes 4194304
  273.4 217.2 %all-gather.6.cloned.1.call-done = f32[8,1,8,512,16]{4,2,0,3,1:T(8,128)} async-done(((f32[1,1,8,512,16]{4,2,0,3,1:T(8,128)}), f32[8,1,8,512,16]{4,2,0,3,1:T(8,128)}) %all-gather.6.cloned.1.call-update) | async-done | bytes 2097168 | tf_op jit(solution)/shard_map/all_gather | solution.py:16
  490.6 10.9 %copy.114 = f32[8,1,8,512,16]{3,4,2,1,0:T(8,128)} copy(f32[8,1,8,512,16]{4,2,0,3,1:T(8,128)} %all-gather.6.cloned.1.call-done) | data formatting | bytes 4194304
  501.5 25.4 %while.34 = (s32[]{:T(128)}, f32[1,8,512,16]{2,3,1,0:T(8,128)S(1)}, f32[1,8,512,16]{2,3,1,0:T(8,128)S(1)}, s32[]{:T(128)}, f32[8]{0:T(128)S(1)}, /*index=5*/f32[...) while((s32[]{:T(128)}, f32[1,8,512,16]{2,3,1,0:T(8,128)S(1)}, ...), condition=%wide.region_1.2_spmd.clone, body=%wide.region_0.1_spmd.clone.sunk | while | flops 659460 | bytes 1622161 | solution.py:29
  533.0 4.0 mul.217
  540.0 19.6 %while.35 = (s32[]{:T(128)}, f32[1,8,512,16]{2,3,1,0:T(8,128)S(1)}, s32[]{:T(128)}, f32[8]{0:T(128)S(1)}, f32[1,8,512,1]{2,1,3,0:T(8,128)S(1)}, /*index=5*/f32[8...) while((s32[]{:T(128)}, f32[1,8,512,16]{2,3,1,0:T(8,128)S(1)}, s32[]{:T(128)}, ...), condition=%wide.region_3.4_spmd.clone, body=%wide.region_2.3_spmd.clone.sunk | while | flops 266248 | bytes 835771 | solution.py:29
  561.6 4.0 multiply_bitcast_fusion
  565.6 10.0 %fusion.19 = f32[512,16,128]{2,1,0:T(8,128)} fusion(f32[128,8,512]{0,1,2:T(8,128)S(1)} %copy-done.7, f32[8,512,16]{2,1,0:T(8,128)S(1)} %get-tuple-element.511), kind=kOutput, calls=%fused_computation.27 | convolution fusion | flops 100663296 | bytes 6553600 | tf_op jit(solution)/shard_map/tmg,bmgi->btgi/dot_general | solution.py:103
  575.6 9.8 %copy.126 = f32[1,128,8192]{2,0,1:T(1,128)} copy(f32[1,128,8192]{1,2,0:T(8,128)} %bitcast.124) | data formatting | bytes 8388608 | tf_op jit(solution)/shard_map/reshape | solution.py:105
  585.5 12.3 %fusion.21 = f32[512,16,128]{2,1,0:T(8,128)} fusion(f32[8,512,16]{2,1,0:T(8,128)S(1)} %copy-done.6, f32[129,8,512]{0,1,2:T(8,128)} %copy-done), kind=kOutput, calls=%fused_computation.29 | convolution fusion | flops 100663296 | bytes 6553600 | tf_op jit(solution)/shard_map/tmg,bmgi->btgi/dot_general | solution.py:100
  597.8 9.8 %copy.117 = f32[1,128,8192]{2,0,1:T(1,128)} copy(f32[1,128,8192]{1,2,0:T(8,128)} %bitcast.125) | data formatting | bytes 8388608 | tf_op jit(solution)/shard_map/reshape | solution.py:102
  607.6 47.8 %fusion.3 = bf16[1,128,8192]{2,0,1:T(2,128)(2,1)} fusion(f32[1,128,8192]{2,0,1:T(1,128)} %copy.126, f32[128,1,8192]{2,1,0:T(1,128)} %copy.119, bf16[1,128,8192]{2,1,0:T(8,128)(2,1)S(1)} %copy-done.16), kind=kOutput, calls=%fused_computation.9 | convolution fusion | flops 407896064 | bytes 12582912 | tf_op jit(solution)/shard_map/conv_general_dilated | solution.py:33
  655.4 46.6 %fusion.4 = bf16[1,128,8192]{2,0,1:T(2,128)(2,1)} fusion(f32[1,128,8192]{2,0,1:T(1,128)S(1)} %copy-done.12, f32[128,1,8192]{2,1,0:T(1,128)S(1)} %copy-done.11, bf16[1,128,8192]{2,1,0:T(8,128)(2,1)S(1)} %copy-done.17), kind=kOutput, calls=%fused_computation.11 | convolution fusion | flops 407896064 | bytes 12582912 | tf_op jit(solution)/shard_map/conv_general_dilated | solution.py:33
  702.1 43.1 %psum.15 = f32[8,512]{0,1:T(8,128)S(1)} all-reduce(f32[8,512]{0,1:T(8,128)S(1)} %multiply_multiply_fusion), channel_id=1, replica_groups=mesh['seq'=8,'batch'=4] {'seq','batch'}, use_global_device_ids=true, to_apply=%region_6.7 | all-reduce | flops 4096 | bytes 32768 | tf_op jit(solution)/shard_map/psum | solution.py:119
  745.9 5.9 copy.137
  751.9 3.6 copy.136
  (141 shorter events, 86.5 us)
Async XLA Ops:
  7.2 255.8 %all-gather.4.cloned.1.call-start = ((), (), s32[]{:S(2)}) async-start(), calls=%async_computation | async-start | bytes 18874368 | tf_op jit(solution)/shard_map/all_gather | solution.py:16
  8.1 3.4 copy-start.13
  8.7 2.7 copy-start
  32.5 458.1 %all-gather.6.cloned.1.call-start = ((), (), s32[]{:S(2)}) async-start(), calls=%async_computation.1 | async-start | bytes 18874368 | tf_op jit(solution)/shard_map/all_gather | solution.py:16
  33.3 506.8 %all-gather.8.cloned.1.call-start = ((), (), s32[]{:S(2)}) async-start(), calls=%async_computation.2 | async-start | bytes 2359296 | tf_op jit(solution)/shard_map/all_gather | solution.py:16
  43.0 8.3 %copy-start.19 = (f32[8,8192]{1,0:T(8,128)S(1)}, f32[8,8192]{1,0:T(8,128)}, u32[]{:S(2)}) copy-start(f32[8,8192]{1,0:T(8,128)} %param.10) | copy-start | bytes 786436
  46.6 4.8 copy-start.8
  47.4 708.1 %all-reduce.3.cloned.1.call-start = ((), (), s32[]{:S(2)}) async-start(), calls=%async_computation.3 | async-start | bytes 524288 | tf_op jit(solution)/shard_map/psum | solution.py:119
  55.4 11.2 %copy-start.23 = (u32[32]{0:T(128)S(1)}, u32[32]{0:T(128)}, u32[]{:S(2)}) copy-start(u32[32]{0:T(128)} %constant.98) | copy-start | bytes 388
  177.4 5.9 copy-start.5
  273.3 228.2 %copy-start.1 = (f32[1,8,512,16]{2,3,1,0:T(8,128)S(1)}, f32[1,8,512,16]{2,3,1,0:T(8,128)}, u32[]{:S(2)}) copy-start(f32[1,8,512,16]{2,3,1,0:T(8,128)} %custom-call) | copy-start | bytes 786436
  273.3 228.2 %copy-start.2 = (f32[1,8,512,16]{2,3,1,0:T(8,128)S(1)}, f32[1,8,512,16]{2,3,1,0:T(8,128)}, u32[]{:S(2)}) copy-start(f32[1,8,512,16]{2,3,1,0:T(8,128)} %custom-call.1) | copy-start | bytes 786436
  273.3 228.1 %copy-start.18 = (f32[1,8,512,1]{2,1,3,0:T(8,128)S(1)}, f32[1,8,512,1]{2,1,3,0:T(8,128)}, u32[]{:S(2)}) copy-start(f32[1,8,512,1]{2,1,3,0:T(8,128)} %copy.112) | copy-start | bytes 49156
  273.3 228.1 %copy-start.22 = (f32[8]{0:T(128)S(1)}, f32[8]{0:T(128)}, u32[]{:S(2)}) copy-start(f32[8]{0:T(128)} %all-reduce) | copy-start | bytes 100
  501.5 27.5 %copy-start.9 = (f32[512,2,8,16]{0,3,2,1:T(8,128)S(1)}, f32[512,2,8,16]{0,3,2,1:T(8,128)}, u32[]{:S(2)}) copy-start(f32[512,2,8,16]{0,3,2,1:T(8,128)} %copy-done.8) | copy-start | bytes 1572868
  501.5 27.4 %copy-start.20 = (f32[8,512,16]{1,2,0:T(8,128)S(1)}, f32[8,512,16]{1,2,0:T(8,128)}, u32[]{:S(2)}) copy-start(f32[8,512,16]{1,2,0:T(8,128)} %copy.134) | copy-start | bytes 786436
  527.0 4.0 copy-start.15
  528.9 11.1 %copy-start.3 = (f32[1,8,512,16]{2,3,1,0:T(8,128)S(1)}, f32[1,8,512,16]{2,3,1,0:T(8,128)}, u32[]{:S(2)}) copy-start(f32[1,8,512,16]{2,3,1,0:T(8,128)} %custom-call.2) | copy-start | bytes 786436
  533.0 28.6 %copy-start.4 = (f32[1,8,512,16]{3,2,1,0:T(8,128)S(1)}, f32[1,8,512,16]{3,2,1,0:T(8,128)}, u32[]{:S(2)}) copy-start(f32[1,8,512,16]{3,2,1,0:T(8,128)} %broadcast_in_dim_reshape.7) | copy-start | bytes 786436
  561.5 4.0 copy-start.7
  575.6 9.8 %copy-start.6 = (f32[8,512,16]{2,1,0:T(8,128)S(1)}, f32[8,512,16]{2,1,0:T(8,128)}, u32[]{:S(2)}) copy-start(f32[8,512,16]{2,1,0:T(8,128)} %get-tuple-element.512) | copy-start | bytes 786436
  597.8 9.8 %copy-start.16 = (bf16[1,128,8192]{2,1,0:T(8,128)(2,1)S(1)}, bf16[1,128,8192]{2,1,0:T(8,128)(2,1)}, u32[]{:S(2)}) copy-start(bf16[1,128,8192]{2,1,0:T(8,128)(2,1)} %param.9) | copy-start | bytes 6291460
  607.6 47.8 %copy-start.11 = (f32[128,1,8192]{2,1,0:T(1,128)S(1)}, f32[128,1,8192]{2,1,0:T(1,128)}, u32[]{:S(2)}) copy-start(f32[128,1,8192]{2,1,0:T(1,128)} %broadcast_in_dim.16) | copy-start | bytes 12582916
  607.6 47.8 %copy-start.12 = (f32[1,128,8192]{2,0,1:T(1,128)S(1)}, f32[1,128,8192]{2,0,1:T(1,128)}, u32[]{:S(2)}) copy-start(f32[1,128,8192]{2,0,1:T(1,128)} %copy.117) | copy-start | bytes 12582916
  607.6 47.8 %copy-start.17 = (bf16[1,128,8192]{2,1,0:T(8,128)(2,1)S(1)}, bf16[1,128,8192]{2,1,0:T(8,128)(2,1)}, u32[]{:S(2)}) copy-start(bf16[1,128,8192]{2,1,0:T(8,128)(2,1)} %param.8) | copy-start | bytes 6291460
  655.4 46.6 %copy-start.14 = (f32[8,512]{0,1:T(8,128)S(1)}, f32[8,512]{0,1:T(8,128)}, u32[]{:S(2)}) copy-start(f32[8,512]{0,1:T(8,128)} %copy-done.13) | copy-start | bytes 49156
  655.4 46.6 %copy-start.21 = (f32[8,512]{0,1:T(8,128)S(1)}, f32[8,512]{0,1:T(8,128)}, u32[]{:S(2)}) copy-start(f32[8,512]{0,1:T(8,128)} %copy.142) | copy-start | bytes 49156
  745.9 6.0 copy-start.10
Sparse Core Ops, SparseCore 0:
  32.6 230.3 all-gather.3
  265.1 225.4 all-gather.5
  492.7 47.2 all-gather.7
  545.4 125.0 all-reduce.2
where the time goes:
time: 775 us; the launch traced here: 764 us
  waiting for transfers between devices  244 us (31%)
  matrix products  213 us (27%)
  local copies, waits for them, and re-layouts  176 us (23%)
  blocking collectives  68 us (9%)
  other arithmetic  47 us (6%)
  between operations  14.3 us (2%)
    all_gather x3, waiting for transfers between devices, carried_in(): everything = jax.tree.map(lambda part: lax.all_gather(part, axis), shard)  243 us
    conv_general_dilated x3, matrix products, depthwise(): lax.conv_general_dilated(values, kernel[:, None, :], (1,), [padding], dim...  156 us
    psum x1, blocking collectives, local(): lax.psum((residue_part.reshape(M, channels) * norm_factor, rate_part * no...  43.1 us
    unnamed x61, local copies, waits for them, and re-layouts  42.5 us
    rev x1, local copies, waits for them, and re-layouts, local(): local_out = depthwise(inputs, kernel[::-1], (length - 1, 0), HIGHER)  32.7 us
    unnamed x1, blocking collectives  24.8 us
    select_n x16, other arithmetic, lap(): return jax.tree.map(lambda a, b: jnp.where(reached, a, b), new, before)  24.2 us
  transfers between devices with their start and end apart: 4, of which 3 were waited for; matrix products, arithmetic and copies ran while one was open for 54% of the time, Pallas kernels for 0%

commit v1 on v0

v1 whole, which is shorter than its diff:
```python
import functools

import jax
import jax.numpy as jnp
import numpy as np
from jax import lax
from jax.experimental import pallas as pl
from jax.experimental.pallas import tpu as pltpu
from jax.sharding import PartitionSpec as P

LANES = 256
F32 = jnp.float32
BF16 = jnp.bfloat16


def split(value):
    high = value.astype(BF16)
    return high, (value - high.astype(F32)).astype(BF16)


def mul(a, b):
    return jnp.dot(a, b, preferred_element_type=F32)


def twice(value, axis):
    return jnp.concatenate([value, value], axis=axis)


def exact_right(left, right):
    return mul(jnp.concatenate(split(left), axis=1), right)


def three(left, right):
    left_high, left_low = split(left)
    right_high, right_low = split(right)
    return mul(left_high, right_high) + (mul(left_low, right_high) + mul(left_high, right_low))


def own_rows(wide, modes, group):
    rows, lanes = wide.shape
    owner = lax.broadcasted_iota(jnp.int32, (modes, lanes), 1) // group
    out = wide[:modes]
    for g in range(1, rows // modes):
        out = jnp.where(owner == g, wide[g * modes : (g + 1) * modes], out)
    return out


def spread(narrow, rows, group):
    modes, lanes = narrow.shape
    owner = lax.broadcasted_iota(jnp.int32, (modes, lanes), 1) // group
    return jnp.concatenate(
        [jnp.where(owner == g, narrow, 0.0) for g in range(rows // modes)], axis=0
    )


def states_kernel(modes, group, rate_ref, x_ref, g_ref, state_ref, weighted_ref):
    length = x_ref.shape[0]
    rate = rate_ref[0]
    at = lax.broadcasted_iota(jnp.int32, (length, rate.shape[1]), 0).astype(F32)
    rising = jnp.exp(-rate * at)
    falling = jnp.exp(-rate * (length - 1.0 - at))
    for k, (table, weight, values) in enumerate(
        ((falling, length - at, x_ref[...]), (rising, at, g_ref[...]))
    ):
        left = jnp.concatenate([table.T, (weight * table).T], axis=0)
        both = exact_right(left, twice(values, 0))
        rows = table.shape[1]
        state_ref[k] = own_rows(both[:rows], modes, group)
        weighted_ref[k] = own_rows(both[rows:], modes, group)


def main_kernel(
    modes, group, rate_ref, pole_ref, gap_ref, dft_ref, inv_high_ref, inv_low_ref, angle_ref,
    x_ref, g_ref, res_ref, rates_ref, state_ref, weighted_ref, carry_ref,
    y_ref, gs_ref, gres_ref, grate_ref,
):
    length = x_ref.shape[0]
    half = length // 2
    rate = rate_ref[0]
    pole = pole_ref[0]
    gap = gap_ref[0]
    gm = rate.shape[1]
    scale = 1.0 / half
    real = gap + pole * angle_ref[0]
    imag = pole * angle_ref[1]
    inverse = 1.0 / (real * real + imag * imag)
    phi_r = real * inverse
    phi_i = -imag * inverse
    psi_r = phi_r * phi_r - phi_i * phi_i - phi_r
    psi_i = 2.0 * phi_r * phi_i - phi_i
    phi = jnp.concatenate([phi_r, phi_i], axis=0)
    phi_t = jnp.concatenate([phi_r, -phi_i], axis=0).T
    psi_t = jnp.concatenate([psi_r, -psi_i], axis=0).T
    x_hat = mul(dft_ref[...], twice(x_ref[...], 0))
    g_hat = mul(dft_ref[...], twice(g_ref[...], 0))
    res = res_ref[...]
    phi_high, phi_low = split(phi)
    res_wide = spread(res, gm, group)
    res_high, res_low = split(res_wide)
    k_hat = mul(jnp.concatenate([phi_high, phi_low], 1), twice(res_high, 0)) + mul(phi_high, res_low)
    xr, xi = x_hat[:half], x_hat[half:]
    gr, gi = g_hat[:half], g_hat[half:]
    kr, ki = k_hat[:half], k_hat[half:]
    y_hat = jnp.concatenate([kr * xr - ki * xi, kr * xi + ki * xr], axis=0)
    h_hat = jnp.concatenate([kr * gr + ki * gi, kr * gi - ki * gr], axis=0)
    lag = jnp.concatenate([gr * xr + gi * xi, gr * xi - gi * xr], axis=0) * scale
    lane_rate = rates_ref[...]
    lane_pole = jnp.exp(-lane_rate)
    whole = jnp.exp(-lane_rate * length)
    fold = 1.0 / (1.0 + whole)
    s_x, s_g = state_ref[0], state_ref[1]
    carry, adjoint = carry_ref[0], carry_ref[1]
    turned_x, turned_g = s_x * fold, s_g * fold
    carry_all = carry + turned_x
    adjoint_all = adjoint + turned_g
    at = lax.broadcasted_iota(jnp.int32, (length, gm), 0).astype(F32)
    rising = jnp.exp(-rate * (at + 1.0))
    falling = jnp.exp(-rate * (length - at))
    for table, hat, start, out in (
        (rising, y_hat, carry_all, y_ref),
        (falling, h_hat, adjoint_all, gs_ref),
    ):
        table_high, table_low = split(table)
        left_high = jnp.concatenate([inv_high_ref[...], table_high], axis=1)
        left_low = jnp.concatenate([inv_low_ref[...], table_low], axis=1)
        right = jnp.concatenate([hat, spread(res * start, gm, group)], axis=0)
        right_high, right_low = split(right)
        total = mul(left_high, right_high) + mul(left_low, right_high) + mul(left_high, right_low)
        out[...] = total.astype(BF16)
    terms = jnp.concatenate([phi_t, psi_t], axis=0)
    terms_high, terms_low = split(terms)
    lag_high, lag_low = split(lag)
    wide = mul(jnp.concatenate([terms_high, terms_low], 1), twice(lag_high, 0)) + mul(
        terms_high, lag_low
    )
    sums = own_rows(wide[:gm], modes, group) + carry_all * lane_pole * s_g
    moments = (
        own_rows(wide[gm:], modes, group)
        + lane_pole * (carry_all * weighted_ref[1] + adjoint_all * weighted_ref[0])
        + length * lane_pole * whole * (carry * adjoint - turned_x * turned_g)
    )
    gres_ref[...] = sums
    rm = -lane_rate * res * moments
    rows = lax.broadcasted_iota(jnp.int32, (LANES, 128), 0) // group
    cols = lax.broadcasted_iota(jnp.int32, (LANES, 128), 1)
    pick = jnp.where(rows == cols, 1.0, 0.0).astype(BF16)
    rm_high, rm_rest = split(rm)
    rm_low = rm_rest
    both = mul(jnp.concatenate([rm_high.astype(F32), rm_low.astype(F32)], 0).astype(BF16), pick)
    grate_ref[0] = both[:modes] + both[modes:]


def constants(length):
    half = length // 2
    omega = np.pi * (2.0 * np.arange(half) + 1.0) / length
    at = np.arange(length)
    forward = np.concatenate([np.cos(np.outer(omega, at)), -np.sin(np.outer(omega, at))], axis=0)
    lanes = np.ones((1, 128))
    angle = np.stack(
        [2.0 * np.sin(omega / 2.0)[:, None] ** 2 * lanes, np.sin(omega)[:, None] * lanes]
    )
    return forward.astype(np.float32), (forward.T / half).astype(np.float32), angle.astype(np.float32)


def local(mesh_shape, signal, out_grad, residues, log_rates):
    batch_rows, length, channels = signal.shape
    modes, groups = log_rates.shape
    group = channels // groups
    blocks = channels // LANES
    gm = LANES // group * modes
    norm = 1.0 / (batch_rows * mesh_shape["batch"] * length * mesh_shape["seq"])
    decay = jnp.exp(log_rates)
    flat = decay.T.reshape(blocks, 1, gm)
    pole = jnp.exp(-flat)
    gap = -jnp.expm1(-flat)
    lane_rate = jnp.repeat(decay, group, axis=1)
    forward, inverse, angle = constants(length)
    dft_high = jnp.asarray(forward).astype(BF16)
    dft = jnp.concatenate(
        [dft_high, (jnp.asarray(forward) - dft_high.astype(F32)).astype(BF16)], axis=1
    )
    inv_high, inv_low = split(jnp.asarray(inverse))
    angle = jnp.asarray(angle)
    peers = mesh_shape["seq"]
    me = lax.axis_index("seq")

    row_spec = pl.BlockSpec((1, 1, gm), lambda b: (b, 0, 0))
    data_spec = pl.BlockSpec((length, LANES), lambda b: (0, b))
    lane_spec = pl.BlockSpec((modes, LANES), lambda b: (0, b))
    pair_spec = pl.BlockSpec((2, modes, LANES), lambda b: (0, 0, b))

    def fixed(shape):
        return pl.BlockSpec(shape, lambda b: (0,) * len(shape))

    pair = jax.ShapeDtypeStruct((2, modes, channels), F32)
    mixed, grads, res_sum, rate_sum = [], [], 0.0, 0.0
    for row in range(batch_rows):
        x, g = signal[row], out_grad[row]
        state, weighted = pl.pallas_call(
            functools.partial(states_kernel, modes, group),
            grid=(blocks,),
            in_specs=[row_spec, data_spec, data_spec],
            out_specs=[pair_spec, pair_spec],
            out_shape=[pair, pair],
        )(flat, x, g)
        every = lax.all_gather(state, "seq")
        order = jnp.arange(peers)
        ahead = (me - 1 - order).astype(F32)[:, None, None]
        behind = (order - me - 1).astype(F32)[:, None, None]
        from_left = jnp.where(ahead >= 0, jnp.exp(-lane_rate * (jnp.maximum(ahead, 0) * length)), 0.0)
        from_right = jnp.where(behind >= 0, jnp.exp(-lane_rate * (jnp.maximum(behind, 0) * length)), 0.0)
        carry = jnp.stack(
            [jnp.sum(from_left * every[:, 0], axis=0), jnp.sum(from_right * every[:, 1], axis=0)]
        )
        y, gs, part, rates = pl.pallas_call(
            functools.partial(main_kernel, modes, group),
            grid=(blocks,),
            in_specs=[
                row_spec, row_spec, row_spec,
                fixed(dft.shape), fixed(inv_high.shape), fixed(inv_low.shape), fixed(angle.shape),
                data_spec, data_spec, lane_spec, lane_spec, pair_spec, pair_spec, pair_spec,
            ],
            out_specs=[
                data_spec, data_spec, lane_spec,
                pl.BlockSpec((1, modes, 128), lambda b: (b, 0, 0)),
            ],
            out_shape=[
                jax.ShapeDtypeStruct((length, channels), BF16),
                jax.ShapeDtypeStruct((length, channels), BF16),
                jax.ShapeDtypeStruct((modes, channels), F32),
                jax.ShapeDtypeStruct((blocks, modes, 128), F32),
            ],
        )(flat, pole, gap, dft, inv_high, inv_low, angle, x, g, residues, lane_rate, state, weighted, carry)
        mixed.append(y)
        grads.append(gs)
        res_sum = res_sum + part
        rate_sum = rate_sum + rates
    rate_sum = rate_sum[:, :, : LANES // group]
    res_sum, rate_sum = lax.psum((res_sum * norm, rate_sum * norm), ("seq", "batch"))
    grad_rates = jnp.swapaxes(rate_sum, 0, 1).reshape(modes, groups)
    return jnp.stack(mixed), jnp.stack(grads), res_sum, grad_rates


def solution(mesh):
    placed = (P("batch", "seq", None), P("batch", "seq", None), P(), P())
    return jax.shard_map(
        functools.partial(local, dict(mesh.shape)),
        mesh=mesh,
        in_specs=placed,
        out_specs=placed,
        check_vma=False,
    )
```

time: 775 us -> 278 us (0.36)
  matrix products: 213 us -> 0 us
  local copies, waits for them, and re-layouts: 176 us -> 5.58 us
  waiting for transfers between devices: 244 us -> 158 us
  Pallas kernels: 0 us -> 50.4 us
  other arithmetic: 47 us -> 7.25 us
  blocking collectives: 68 us -> 38.9 us
    all_gather x3 -> x1, waiting for transfers between devices: 243 us -> 72.7 us  [local(): every = lax.all_gather(state, 'seq')]
    conv_general_dilated x3 -> x0, matrix products: 156 us -> none  [depthwise(): lax.conv_general_dilated(values, kernel[:, None, :], (1,), [padding], dim...]
    psum x1, waiting for transfers between devices: 0.01 us -> 85.3 us  [local(): lax.psum((res_sum * norm, rate_sum * norm), ('seq', 'batch'))]
    dot_general x6 -> x0, matrix products: 56.7 us -> none  [the longest x1 12.3 us: local(): jnp.einsum('tmg,bmgi->btgi', powers[1:], res_group[None] * carry_state, p...]
    pallas_call x0 -> x2, Pallas kernels: none -> 50.4 us  [the longest x1 29.9 us: local(): pl.pallas_call(functools.partial(main_kernel, modes, group), grid=(blocks...]
    rev x3 -> x0, local copies, waits for them, and re-layouts: 42.3 us -> none  [the longest x1 32.7 us: local(): local_out = depthwise(inputs, kernel[::-1], (length - 1, 0), HIGHER)]
    unnamed x61 -> x5, local copies, waits for them, and re-layouts: 42.5 us -> 1.68 us
    unnamed x1 -> x0, blocking collectives: 24.8 us -> none
  transfers between devices with their start and end apart: 4 -> 2, of which waited for: 3 -> 2; matrix products, arithmetic and copies ran while one was open for 54% -> 1% of each run, Pallas kernels for 0% -> 0%
where the time goes in v1:
time: 278 us; the launch traced here: 274 us
  waiting for transfers between devices  158 us (57%)
  Pallas kernels  50.4 us (18%)
  blocking collectives  38.9 us (14%)
  between operations  14.1 us (5%)
  other arithmetic  7.25 us (3%)
  local copies, waits for them, and re-layouts  5.58 us (2%)
    psum x1, waiting for transfers between devices, local(): lax.psum((res_sum * norm, rate_sum * norm), ('seq', 'batch'))  85.3 us
    all_gather x1, waiting for transfers between devices, local(): every = lax.all_gather(state, 'seq')  72.7 us
    psum x1, blocking collectives, local(): lax.psum((res_sum * norm, rate_sum * norm), ('seq', 'batch'))  38.9 us
    pallas_call x1, Pallas kernels, local(): pl.pallas_call(functools.partial(main_kernel, modes, group), grid=(blocks...  29.9 us
    pallas_call x1, Pallas kernels, local(): pl.pallas_call(functools.partial(states_kernel, modes, group), grid=(bloc...  20.5 us
  transfers between devices with their start and end apart: 2, of which 2 were waited for; matrix products, arithmetic and copies ran while one was open for 1% of the time, Pallas kernels for 0%

profile of v1, /device:TPU:0, one launch (start us, length us, event | category | flops | bytes accessed | tf_op | source)
XLA Modules:
  0.0 274.5 jit_solution(17041183273270924825)
XLA Ops:
  7.2 0.0 all-gather.3.cloned.1.call-start
  7.2 0.7 fusion.4
  7.9 0.1 copy.25
  8.1 0.8 reshape.77
  8.8 0.0 copy-start.1
  8.8 20.5 %shard_map.102 = (f32[2,8,8192]{2,1,0:T(8,128)}, f32[2,8,8192]{2,1,0:T(8,128)}) custom-call(f32[32,1,128]{2,1,0:T(1,128)} %bitcast.37, bf16[128,8192]{1,0:T(8,128)(2,1)} %bitcast.30, bf16[128,8192]{1,0:T(8,128)(2,1)} %bitcast.32), custom_call_target="tpu_custom_call" | custom-call | tf_op jit(solution)/shard_map/pallas_call | solution.py:199
  29.3 0.0 all-gather.3.cloned.1.call-update
  29.4 0.0 all-reduce.2.cloned.1.call-start
  29.4 0.0 copy-done.1
  29.4 0.6 broadcast_in_dim.25
  30.0 1.6 reshape.78.rates_ref
  31.6 0.0 copy-start
  31.7 0.6 exponential-minus-one_negate_fusion
  32.3 72.7 %all-gather.3.cloned.1.call-done = f32[16,8,8192]{2,1,0:T(8,128)} async-done(((f32[2,8,8192]{2,1,0:T(8,128)}), f32[16,8,8192]{2,1,0:T(8,128)}) %all-gather.3.cloned.1.call-update) | async-done | bytes 4194320 | tf_op jit(solution)/shard_map/all_gather | solution.py:206
  105.0 3.2 %fusion.3 = (f32[8,8192]{1,0:T(8,128)S(1)}, f32[8,8192]{1,0:T(8,128)S(1)}) fusion(f32[8,2,8,8192]{3,2,1,0:T(8,128)} %bitcast.34, f32[8]{0:T(128)S(1)} %get-tuple-element.23, f32[8,8192]{1,0:T(8,128)S(1)} %neg.29, pred[8]{0:T(512)(128)(4,1)S(1)} %get-tuple-element.25, f32[8]{0:T(128)S(1)} %get-tuple-element.22, pred[8]{0:T(512)(128)(4,1)S(1)} %get-tuple-element.24), kind=kLoop, calls=%fused_computation.5 | loop fusion | flops 4063232 | bytes 4980816 | tf_op jit(solution)/shard_map/reduce_sum | solution.py:213
  108.2 0.0 copy-done
  108.2 0.8 pad_maximum_fusion.carry_ref
  109.0 29.9 %shard_map.103 = (bf16[128,8192]{1,0:T(8,128)(2,1)}, bf16[128,8192]{1,0:T(8,128)(2,1)}, f32[8,8192]{1,0:T(8,128)}, f32[32,8,128]{2,1,0:T(8,128)}) custom-call(f32[32,1,128]{2,1,0:T(1,128)} %bitcast.38, f32[32,1,128]{2,1,0:T(1,128)} %bitcast.40, f32[32,1,128]{2,1,0:T(1,128)} %bitcast.39, bf16[128,256]{1,0:T(8,128)(2,1)} %constant.34.dft_ref, ...), custom_call_target="tpu_custom_call" | custom-call | tf_op jit(solution)/shard_map/pallas_call | solution.py:215
  138.9 1.7 broadcast_multiply_fusion
  140.6 0.0 all-reduce.2.cloned.1.call-update
  140.6 0.9 multiply_bitcast_fusion
  141.6 0.1 reshape.79
  141.7 38.9 %psum.15 = f32[8,512]{1,0:T(8,128)} all-reduce(f32[8,512]{1,0:T(8,128)S(1)} %reshape.79), channel_id=1, replica_groups=mesh['seq'=8,'batch'=4] {'seq','batch'}, use_global_device_ids=true, to_apply=%region_3.4 | all-reduce | flops 4096 | bytes 32768 | tf_op jit(solution)/shard_map/psum | solution.py:239
  180.6 85.3 %all-reduce.2.cloned.1.call-done = f32[8,8192]{1,0:T(8,128)} async-done(((f32[8,8192]{1,0:T(8,128)}), f32[8,8192]{1,0:T(8,128)}) %all-reduce.2.cloned.1.call-update) | async-done | bytes 262160 | tf_op jit(solution)/shard_map/psum | solution.py:239
  266.0 1.7 copy.34
  (5 shorter events, 0.1 us)
Async XLA Ops:
  7.2 97.9 %all-gather.3.cloned.1.call-start = ((), (), s32[]{:S(2)}) async-start(), calls=%async_computation.1 | async-start | bytes 4718592 | tf_op jit(solution)/shard_map/all_gather | solution.py:206
  8.8 20.6 %copy-start.1 = (f32[32,1,128]{2,0,1:T(8,128)S(1)}, f32[32,1,128]{2,0,1:T(8,128)}, u32[]{:S(2)}) copy-start(f32[32,1,128]{2,0,1:T(8,128)} %reshape.77) | copy-start | bytes 49156
  29.4 236.6 %all-reduce.2.cloned.1.call-start = ((), (), s32[]{:S(2)}) async-start(), calls=%async_computation | async-start | bytes 524288 | tf_op jit(solution)/shard_map/psum | solution.py:239
  31.6 76.6 %copy-start = (f32[8,8192]{1,0:T(8,128)}, f32[8,8192]{1,0:T(8,128)S(1)}, u32[]{:S(2)}) copy-start(f32[8,8192]{1,0:T(8,128)S(1)} %reshape.78.rates_ref) | copy-start | bytes 786436
Sparse Core Ops, SparseCore 0:
  29.5 75.5 all-gather.2
  140.7 125.1 all-reduce.1

commit v2 on v1

--- a/solution.py
+++ b/solution.py
@@ -11,6 +11,9 @@
 LANES = 256
 F32 = jnp.float32
 BF16 = jnp.bfloat16
+MESH = pl.DeviceIdType.MESH
+STATE_SUB = 4
+MAIN_SUB = 2
 
 
 def split(value):
@@ -55,18 +58,20 @@
 
 def states_kernel(modes, group, rate_ref, x_ref, g_ref, state_ref, weighted_ref):
     length = x_ref.shape[0]
-    rate = rate_ref[0]
-    at = lax.broadcasted_iota(jnp.int32, (length, rate.shape[1]), 0).astype(F32)
-    rising = jnp.exp(-rate * at)
-    falling = jnp.exp(-rate * (length - 1.0 - at))
-    for k, (table, weight, values) in enumerate(
-        ((falling, length - at, x_ref[...]), (rising, at, g_ref[...]))
-    ):
-        left = jnp.concatenate([table.T, (weight * table).T], axis=0)
-        both = exact_right(left, twice(values, 0))
-        rows = table.shape[1]
-        state_ref[k] = own_rows(both[:rows], modes, group)
-        weighted_ref[k] = own_rows(both[rows:], modes, group)
+    for j in range(rate_ref.shape[0]):
+        lanes = slice(j * LANES, (j + 1) * LANES)
+        rate = rate_ref[j]
+        at = lax.broadcasted_iota(jnp.int32, (length, rate.shape[1]), 0).astype(F32)
+        rising = jnp.exp(-rate * at)
+        falling = jnp.exp(-rate * (length - 1.0 - at))
+        for k, (table, weight, values) in enumerate(
+            ((falling, length - at, x_ref[:, lanes]), (rising, at, g_ref[:, lanes]))
+        ):
+            left = jnp.concatenate([table.T, (weight * table).T], axis=0)
+            both = exact_right(left, twice(values, 0))
+            rows = table.shape[1]
+            state_ref[k, :, lanes] = own_rows(both[:rows], modes, group)
+            weighted_ref[k, :, lanes] = own_rows(both[rows:], modes, group)
 
 
 def main_kernel(
@@ -74,11 +79,27 @@
     x_ref, g_ref, res_ref, rates_ref, state_ref, weighted_ref, carry_ref,
     y_ref, gs_ref, gres_ref, grate_ref,
 ):
+    sub = rate_ref.shape[0]
+    for j in range(sub):
+        lanes = slice(j * LANES, (j + 1) * LANES)
+        main_block(
+            modes, group, j, rate_ref, pole_ref, gap_ref, dft_ref, inv_high_ref, inv_low_ref, angle_ref,
+            x_ref.at[:, lanes], g_ref.at[:, lanes], res_ref.at[:, lanes], rates_ref.at[:, lanes],
+            state_ref.at[:, :, lanes], weighted_ref.at[:, :, lanes], carry_ref.at[:, :, lanes],
+            y_ref.at[:, lanes], gs_ref.at[:, lanes], gres_ref.at[:, lanes], grate_ref,
+        )
+
+
+def main_block(
+    modes, group, j, rate_ref, pole_ref, gap_ref, dft_ref, inv_high_ref, inv_low_ref, angle_ref,
+    x_ref, g_ref, res_ref, rates_ref, state_ref, weighted_ref, carry_ref,
+    y_ref, gs_ref, gres_ref, grate_ref,
+):
     length = x_ref.shape[0]
     half = length // 2
-    rate = rate_ref[0]
-    pole = pole_ref[0]
-    gap = gap_ref[0]
+    rate = rate_ref[j]
+    pole = pole_ref[j]
+    gap = gap_ref[j]
     gm = rate.shape[1]
     scale = 1.0 / half
     real = gap + pole * angle_ref[0]
@@ -141,13 +162,129 @@
     )
     gres_ref[...] = sums
     rm = -lane_rate * res * moments
+    sub = rate_ref.shape[0]
+    per = LANES // group
+    step = lax.rem(pl.program_id(0) * sub + j, 128 // per)
     rows = lax.broadcasted_iota(jnp.int32, (LANES, 128), 0) // group
     cols = lax.broadcasted_iota(jnp.int32, (LANES, 128), 1)
-    pick = jnp.where(rows == cols, 1.0, 0.0).astype(BF16)
-    rm_high, rm_rest = split(rm)
-    rm_low = rm_rest
-    both = mul(jnp.concatenate([rm_high.astype(F32), rm_low.astype(F32)], 0).astype(BF16), pick)
-    grate_ref[0] = both[:modes] + both[modes:]
+    pick = jnp.where(rows + step * per == cols, 1.0, 0.0).astype(BF16)
+    both = mul(jnp.concatenate(split(rm), 0), pick)
+    added = both[:modes] + both[modes:]
+    if j == 0:
+        @pl.when(step == 0)
+        def _():
+            grate_ref[...] = jnp.zeros_like(grate_ref)
+    grate_ref[...] += added
+
+
+def barrier_with(peers):
+    barrier = pltpu.get_barrier_semaphore()
+    for axis, peer in peers:
+        pl.semaphore_signal(barrier, inc=1, device_id={axis: peer}, device_id_type=MESH)
+    pl.semaphore_wait(barrier, len(peers))
+
+
+def send(source, target, send_sem, recv_sem, axis, peer):
+    copy = pltpu.make_async_remote_copy(
+        src_ref=source, dst_ref=target, send_sem=send_sem, recv_sem=recv_sem,
+        device_id={axis: peer}, device_id_type=MESH,
+    )
+    copy.start()
+    return copy
+
+
+def carry_kernel(
+    n, length, state_ref, rate_ref, out_ref, inbox, outbox, landed, send_a, recv_a, send_b, recv_b
+):
+    me = lax.axis_index("seq")
+    width = state_ref.shape[2] // n
+    others = [lax.rem(me + k, n) for k in range(1, n)]
+
+    def lanes(index):
+        return pl.ds(pl.multiple_of(index * width, 128), width)
+
+    barrier_with([("seq", peer) for peer in others])
+    first = [
+        send(state_ref.at[:, :, lanes(peer)], inbox.at[me], send_a.at[k], recv_a.at[k], "seq", peer)
+        for k, peer in enumerate(others)
+    ]
+    inbox[me] = state_ref[:, :, lanes(me)]
+    whole = jnp.exp(-rate_ref[:, lanes(me)] * length)
+    for copy in first:
+        copy.wait_recv()
+    carry = jnp.zeros_like(whole)
+    adjoint = jnp.zeros_like(whole)
+    for i in range(n):
+        outbox[i, 0] = carry
+        carry = inbox[i, 0] + whole * carry
+        last = n - 1 - i
+        outbox[last, 1] = adjoint
+        adjoint = inbox[last, 1] + whole * adjoint
+    second = [
+        send(outbox.at[peer], landed.at[:, :, lanes(me)], send_b.at[k], recv_b.at[k], "seq", peer)
+        for k, peer in enumerate(others)
+    ]
+    landed[:, :, lanes(me)] = outbox[me]
+    for copy in second:
+        copy.wait_recv()
+    out_ref[...] = landed[...]
+    for copy in first + second:
+        copy.wait_send()
+
+
+def reduce_kernel(
+    n, rows, norm, res_ref, rate_ref, res_out, rate_out, inbox, inrate, rowbox, rowrate, landed,
+    send_a, recv_a, send_b, recv_b, send_c, recv_c, send_d, recv_d, send_e, recv_e,
+):
+    me = lax.axis_index("seq")
+    mine = lax.axis_index("batch")
+    width = res_ref.shape[1] // n
+    others = [lax.rem(me + k, n) for k in range(1, n)]
+    beside = [lax.rem(mine + k, rows) for k in range(1, rows)]
+
+    def lanes(index):
+        return pl.ds(pl.multiple_of(index * width, 128), width)
+
+    barrier_with([("seq", peer) for peer in others] + [("batch", peer) for peer in beside])
+    copies = []
+    for k, peer in enumerate(others):
+        copies += [
+            send(res_ref.at[:, lanes(peer)], inbox.at[me], send_a.at[k], recv_a.at[k], "seq", peer),
+            send(rate_ref, inrate.at[me], send_b.at[k], recv_b.at[k], "seq", peer),
+        ]
+    inbox[me] = res_ref[:, lanes(me)]
+    inrate[me] = rate_ref[...]
+    for copy in copies:
+        copy.wait_recv()
+    part, rate_part = inbox[0], inrate[0]
+    for i in range(1, n):
+        part = part + inbox[i]
+        rate_part = rate_part + inrate[i]
+    rowbox[mine] = part
+    rowrate[mine] = rate_part
+    across = []
+    for k, peer in enumerate(beside):
+        across += [
+            send(rowbox.at[mine], rowbox.at[mine], send_c.at[k], recv_c.at[k], "batch", peer),
+            send(rowrate.at[mine], rowrate.at[mine], send_d.at[k], recv_d.at[k], "batch", peer),
+        ]
+    for copy in across:
+        copy.wait_recv()
+    part, rate_part = rowbox[0], rowrate[0]
+    for i in range(1, rows):
+        part = part + rowbox[i]
+        rate_part = rate_part + rowrate[i]
+    landed[:, lanes(me)] = part * norm
+    back = [
+        send(landed.at[:, lanes(me)], landed.at[:, lanes(me)], send_e.at[k], recv_e.at[k], "seq", peer)
+        for k, peer in enumerate(others)
+    ]
+    rate_out[...] = rate_part * norm
+    for copy in back:
+        copy.wait_recv()
+    res_out[...] = landed[...]
+    for copy in copies + across + back:
+        copy.wait_send()
 
 
 def constants(length):
@@ -181,40 +318,54 @@
     )
     inv_high, inv_low = split(jnp.asarray(inverse))
     angle = jnp.asarray(angle)
-    peers = mesh_shape["seq"]
-    me = lax.axis_index("seq")
-
-    row_spec = pl.BlockSpec((1, 1, gm), lambda b: (b, 0, 0))
-    data_spec = pl.BlockSpec((length, LANES), lambda b: (0, b))
-    lane_spec = pl.BlockSpec((modes, LANES), lambda b: (0, b))
-    pair_spec = pl.BlockSpec((2, modes, LANES), lambda b: (0, 0, b))
+    peers, rows = mesh_shape["seq"], mesh_shape["batch"]
+    width = channels // peers
+    lane_pick = 128 // (LANES // group)
+
+    def specs(sub):
+        return (
+            pl.BlockSpec((sub, 1, gm), lambda b: (b, 0, 0)),
+            pl.BlockSpec((length, sub * LANES), lambda b: (0, b)),
+            pl.BlockSpec((modes, sub * LANES), lambda b: (0, b)),
+            pl.BlockSpec((2, modes, sub * LANES), lambda b: (0, 0, b)),
+        )
 
     def fixed(shape):
         return pl.BlockSpec(shape, lambda b: (0,) * len(shape))
 
+    def dma(count):
+        return pltpu.SemaphoreType.DMA((max(count, 1),))
+
+    vmem = pl.BlockSpec(memory_space=pltpu.VMEM)
     pair = jax.ShapeDtypeStruct((2, modes, channels), F32)
     mixed, grads, res_sum, rate_sum = [], [], 0.0, 0.0
     for row in range(batch_rows):
         x, g = signal[row], out_grad[row]
+        row_spec, data_spec, lane_spec, pair_spec = specs(STATE_SUB)
         state, weighted = pl.pallas_call(
             functools.partial(states_kernel, modes, group),
-            grid=(blocks,),
+            grid=(blocks // STATE_SUB,),
             in_specs=[row_spec, data_spec, data_spec],
             out_specs=[pair_spec, pair_spec],
             out_shape=[pair, pair],
         )(flat, x, g)
-        every = lax.all_gather(state, "seq")
-        order = jnp.arange(peers)
-        ahead = (me - 1 - order).astype(F32)[:, None, None]
-        behind = (order - me - 1).astype(F32)[:, None, None]
-        from_left = jnp.where(ahead >= 0, jnp.exp(-lane_rate * (jnp.maximum(ahead, 0) * length)), 0.0)
-        from_right = jnp.where(behind >= 0, jnp.exp(-lane_rate * (jnp.maximum(behind, 0) * length)), 0.0)
-        carry = jnp.stack(
-            [jnp.sum(from_left * every[:, 0], axis=0), jnp.sum(from_right * every[:, 1], axis=0)]
-        )
+        carry = pl.pallas_call(
+            functools.partial(carry_kernel, peers, float(length)),
+            in_specs=[vmem, vmem],
+            out_specs=vmem,
+            out_shape=pair,
+            scratch_shapes=[
+                pltpu.VMEM((peers, 2, modes, width), F32),
+                pltpu.VMEM((peers, 2, modes, width), F32),
+                pltpu.VMEM((2, modes, channels), F32),
+            ]
+            + [dma(peers - 1)] * 4,
+            compiler_params=pltpu.CompilerParams(collective_id=0, has_side_effects=True),
+        )(state, lane_rate)
+        row_spec, data_spec, lane_spec, pair_spec = specs(MAIN_SUB)
         y, gs, part, rates = pl.pallas_call(
             functools.partial(main_kernel, modes, group),
-            grid=(blocks,),
+            grid=(blocks // MAIN_SUB,),
             in_specs=[
                 row_spec, row_spec, row_spec,
                 fixed(dft.shape), fixed(inv_high.shape), fixed(inv_low.shape), fixed(angle.shape),
@@ -222,23 +373,38 @@
             ],
             out_specs=[
                 data_spec, data_spec, lane_spec,
-                pl.BlockSpec((1, modes, 128), lambda b: (b, 0, 0)),
+                pl.BlockSpec((modes, 128), lambda b: (0, b * MAIN_SUB // lane_pick)),
             ],
             out_shape=[
                 jax.ShapeDtypeStruct((length, channels), BF16),
                 jax.ShapeDtypeStruct((length, channels), BF16),
                 jax.ShapeDtypeStruct((modes, channels), F32),
-                jax.ShapeDtypeStruct((blocks, modes, 128), F32),
+                jax.ShapeDtypeStruct((modes, groups), F32),
             ],
         )(flat, pole, gap, dft, inv_high, inv_low, angle, x, g, residues, lane_rate, state, weighted, carry)
         mixed.append(y)
         grads.append(gs)
-        res_sum = res_sum + part
-        rate_sum = rate_sum + rates
-    rate_sum = rate_sum[:, :, : LANES // group]
-    res_sum, rate_sum = lax.psum((res_sum * norm, rate_sum * norm), ("seq", "batch"))
-    grad_rates = jnp.swapaxes(rate_sum, 0, 1).reshape(modes, groups)
-    return jnp.stack(mixed), jnp.stack(grads), res_sum, grad_rates
+        res_sum = res_sum + part if row else part
+        rate_sum = rate_sum + rates if row else rates
+    res_sum, rate_sum = pl.pallas_call(
+        functools.partial(reduce_kernel, peers, rows, norm),
+        in_specs=[vmem, vmem],
+        out_specs=[vmem, vmem],
+        out_shape=[
+            jax.ShapeDtypeStruct((modes, channels), F32),
+            jax.ShapeDtypeStruct((modes, groups), F32),
+        ],
+        scratch_shapes=[
+            pltpu.VMEM((peers, modes, width), F32),
+            pltpu.VMEM((peers, modes, groups), F32),
+            pltpu.VMEM((rows, modes, width), F32),
+            pltpu.VMEM((rows, modes, groups), F32),
+            pltpu.VMEM((modes, channels), F32),
+        ]
+        + [dma(peers - 1)] * 4 + [dma(rows - 1)] * 4 + [dma(peers - 1)] * 2,
+        compiler_params=pltpu.CompilerParams(collective_id=1, has_side_effects=True),
+    )(res_sum, rate_sum)
+    return jnp.stack(mixed), jnp.stack(grads), res_sum, rate_sum
 
 
 def solution(mesh):

time: 278 us -> 103 us (0.37)
  waiting for transfers between devices: 158 us -> 0 us
  Pallas kernels: 50.4 us -> 93.9 us
  blocking collectives: 38.9 us -> 0 us
  between operations: 14.1 us -> 0.68 us
  other arithmetic: 7.25 us -> 0.63 us
    psum x1 -> x0, waiting for transfers between devices: 85.3 us -> none  [local(): lax.psum((res_sum * norm, rate_sum * norm), ('seq', 'batch'))]
    all_gather x1 -> x0, waiting for transfers between devices: 72.7 us -> none  [local(): every = lax.all_gather(state, 'seq')]
    pallas_call x0 -> x2, Pallas kernels: none -> 58.8 us  [the longest x1 30.4 us: local(): pl.pallas_call(functools.partial(carry_kernel, peers, float(length)), in_...]
    psum x1 -> x0, blocking collectives: 38.9 us -> none  [local(): lax.psum((res_sum * norm, rate_sum * norm), ('seq', 'batch'))]
    pallas_call x1, Pallas kernels: 20.5 us -> 7.64 us  [local(): pl.pallas_call(functools.partial(states_kernel, modes, group), grid=(bloc...]
    reduce_sum x1 -> x0, other arithmetic: 3.16 us -> none  [local(): jnp.sum(from_left * every[:, 0], axis=0)]
  transfers between devices with their start and end apart: 2 -> 0, of which waited for: 2 -> 0; matrix products, arithmetic and copies ran while one was open for 1% -> 0% of each run, Pallas kernels for 0% -> 0%
where the time goes in v2:
time: 103 us; the launch traced here: 102 us
  Pallas kernels  93.9 us (91%)
  local copies, waits for them, and re-layouts  6.86 us (7%)
    pallas_call x1, Pallas kernels, local(): pl.pallas_call(functools.partial(carry_kernel, peers, float(length)), in_...  30.4 us
    pallas_call x1, Pallas kernels, local(): pl.pallas_call(functools.partial(reduce_kernel, peers, rows, norm), in_sp...  28.4 us
    pallas_call x1, Pallas kernels, local(): pl.pallas_call(functools.partial(main_kernel, modes, group), grid=(blocks...  27.5 us
    pallas_call x1, Pallas kernels, local(): pl.pallas_call(functools.partial(states_kernel, modes, group), grid=(bloc...  7.64 us
    unnamed x4, local copies, waits for them, and re-layouts  3 us
    reshape x1, local copies, waits for them, and re-layouts, local(): lane_rate = jnp.repeat(decay, group, axis=1)  2.26 us

profile of v2, /device:TPU:0, one launch (start us, length us, event | category | flops | bytes accessed | tf_op | source)
XLA Modules:
  0.0 102.1 jit_solution(11903243420649729270)
XLA Ops:
  0.6 0.7 fusion
  1.4 0.1 copy.16
  1.5 0.2 reshape.42
  1.6 0.0 copy-start
  1.7 0.6 exponential-minus-one_negate_fusion
  2.3 0.0 copy-done
  2.3 7.6 %shard_map.102 = (f32[2,8,8192]{2,1,0:T(8,128)}, f32[2,8,8192]{2,1,0:T(8,128)}) custom-call(f32[32,1,128]{2,1,0:T(1,128)} %bitcast.15, bf16[128,8192]{1,0:T(8,128)(2,1)} %bitcast.11, bf16[128,8192]{1,0:T(8,128)(2,1)} %bitcast.13), custom_call_target="tpu_custom_call" | custom-call | tf_op jit(solution)/shard_map/pallas_call | solution.py:345
  9.9 0.6 broadcast_in_dim.3
  10.5 2.3 %reshape.43.rate_ref.rates_ref = f32[8,8192]{1,0:T(8,128)} reshape(f32[8,512,16]{2,1,0:T(8,128)S(1)} %broadcast_in_dim.3) | data formatting | bytes 524288 | tf_op jit(solution)/shard_map/reshape | solution.py:313
  12.8 30.4 %shard_map.103.carry_ref = f32[2,8,8192]{2,1,0:T(8,128)} custom-call(f32[2,8,8192]{2,1,0:T(8,128)} %get-tuple-element.12.state_ref, f32[8,8192]{1,0:T(8,128)} %reshape.43.rate_ref.rates_ref), custom_call_target="tpu_custom_call" | custom-call | tf_op jit(solution)/shard_map/pallas_call | solution.py:352
  43.2 27.5 %shard_map.104 = (bf16[128,8192]{1,0:T(8,128)(2,1)}, bf16[128,8192]{1,0:T(8,128)(2,1)}, f32[8,8192]{1,0:T(8,128)}, f32[8,512]{1,0:T(8,128)}) custom-call(f32[32,1,128]{2,1,0:T(1,128)} %bitcast.16, f32[32,1,128]{2,1,0:T(1,128)} %bitcast.18, f32[32,1,128]{2,1,0:T(1,128)} %bitcast.17, bf16[128,256]{1,0:T(8,128)(2,1)} %constant.15.dft_ref, ...), custom_call_target="tpu_custom_call" | custom-call | tf_op jit(solution)/shard_map/pallas_call | solution.py:366
  70.7 28.4 %shard_map.105 = (f32[8,8192]{1,0:T(8,128)}, f32[8,512]{1,0:T(8,128)}) custom-call(f32[8,8192]{1,0:T(8,128)} %get-tuple-element.16.res_ref, f32[8,512]{1,0:T(8,128)} %get-tuple-element.17.rate_ref), custom_call_target="tpu_custom_call" | custom-call | tf_op jit(solution)/shard_map/pallas_call | solution.py:389
  99.1 1.7 %copy.23 = f32[8,8192]{1,0:T(8,128)} copy(f32[8,8192]{1,0:T(8,128)} %get-tuple-element.32) | data formatting | bytes 524288
  100.8 1.3 %copy.24 = f32[8,512]{1,0:T(8,128)} copy(f32[8,512]{1,0:T(8,128)} %get-tuple-element.33) | data formatting | bytes 32768
  (1 shorter events, 0.0 us)
Async XLA Ops:
  1.6 0.7 copy-start

commit v3 on v1

v3 whole, which is shorter than its diff:
```python
import functools

import jax
import jax.numpy as jnp
import numpy as np
from jax import lax
from jax.experimental import pallas as pl
from jax.experimental.pallas import tpu as pltpu
from jax.sharding import PartitionSpec as P

LANES = 256
F32 = jnp.float32
BF16 = jnp.bfloat16
MESH = pl.DeviceIdType.MESH
STATE_SUB = 4
MAIN_SUB = 2


def split(value):
    high = value.astype(BF16)
    return high, (value - high.astype(F32)).astype(BF16)


def mul(a, b):
    return jnp.dot(a, b, preferred_element_type=F32)


def twice(value, axis):
    return jnp.concatenate([value, value], axis=axis)


def exact_right(left, right):
    return mul(jnp.concatenate(split(left), axis=1), right)


def own_rows(wide, modes, group):
    rows, lanes = wide.shape
    owner = lax.broadcasted_iota(jnp.int32, (modes, lanes), 1) // group
    out = wide[:modes]
    for g in range(1, rows // modes):
        out = jnp.where(owner == g, wide[g * modes : (g + 1) * modes], out)
    return out


def spread(narrow, rows, group):
    modes, lanes = narrow.shape
    owner = lax.broadcasted_iota(jnp.int32, (modes, lanes), 1) // group
    return jnp.concatenate(
        [jnp.where(owner == g, narrow, 0.0) for g in range(rows // modes)], axis=0
    )


def states_kernel(modes, group, rate_ref, x_ref, g_ref, state_ref, weighted_ref):
    length = x_ref.shape[0]
    for j in range(rate_ref.shape[0]):
        lanes = slice(j * LANES, (j + 1) * LANES)
        rate = rate_ref[j]
        at = lax.broadcasted_iota(jnp.int32, (length, rate.shape[1]), 0).astype(F32)
        rising = jnp.exp(-rate * at)
        falling = jnp.exp(-rate * (length - 1.0 - at))
        for k, (table, weight, values) in enumerate(
            ((falling, length - at, x_ref[:, lanes]), (rising, at, g_ref[:, lanes]))
        ):
            left = jnp.concatenate([table.T, (weight * table).T], axis=0)
            both = exact_right(left, twice(values, 0))
            rows = table.shape[1]
            state_ref[k, :, lanes] = own_rows(both[:rows], modes, group)
            weighted_ref[k, :, lanes] = own_rows(both[rows:], modes, group)


def nega_block(
    modes, group, pole, gap, dft, inv_high, inv_low, angle, x, g, res,
):
    half = x.shape[0] // 2
    gm = pole.shape[1]
    real = gap + pole * angle[0]
    imag = pole * angle[1]
    inverse = 1.0 / (real * real + imag * imag)
    phi_r = real * inverse
    phi_i = -imag * inverse
    psi_r = phi_r * phi_r - phi_i * phi_i - phi_r
    psi_i = 2.0 * phi_r * phi_i - phi_i
    phi = jnp.concatenate([phi_r, phi_i], axis=0)
    phi_t = jnp.concatenate([phi_r, -phi_i], axis=0).T
    psi_t = jnp.concatenate([psi_r, -psi_i], axis=0).T
    x_hat = mul(dft, twice(x, 0))
    g_hat = mul(dft, twice(g, 0))
    phi_high, phi_low = split(phi)
    res_high, res_low = split(spread(res, gm, group))
    k_hat = mul(jnp.concatenate([phi_high, phi_low], 1), twice(res_high, 0)) + mul(phi_high, res_low)
    xr, xi = x_hat[:half], x_hat[half:]
    gr, gi = g_hat[:half], g_hat[half:]
    kr, ki = k_hat[:half], k_hat[half:]
    y_hat = jnp.concatenate([kr * xr - ki * xi, kr * xi + ki * xr], axis=0)
    h_hat = jnp.concatenate([kr * gr + ki * gi, kr * gi - ki * gr], axis=0)
    lag = jnp.concatenate([gr * xr + gi * xi, gr * xi - gi * xr], axis=0) * (1.0 / half)
    inv_both = jnp.concatenate([inv_high, inv_low], axis=1)
    outs = []
    for hat in (y_hat, h_hat):
        hat_high, hat_low = split(hat)
        outs.append(mul(inv_both, twice(hat_high, 0)) + mul(inv_high, hat_low))
    terms_high, terms_low = split(jnp.concatenate([phi_t, psi_t], axis=0))
    lag_high, lag_low = split(lag)
    wide = mul(jnp.concatenate([terms_high, terms_low], 1), twice(lag_high, 0)) + mul(
        terms_high, lag_low
    )
    return outs + [own_rows(wide[:gm], modes, group), own_rows(wide[gm:], modes, group)]


def carry_block(group, table, start):
    high, low = split(table)
    start_high, start_low = split(spread(start, table.shape[1], group))
    return mul(jnp.concatenate([high, low], 1), twice(start_high, 0)) + mul(high, start_low)


def remote(source, target, sems, k, axis, peer):
    return pltpu.make_async_remote_copy(
        src_ref=source, dst_ref=target, send_sem=sems[0].at[k], recv_sem=sems[1].at[k],
        device_id={axis: peer}, device_id_type=MESH,
    )


def whole_kernel(
    n, rows, norm, modes, group, steps,
    rate_ref, pole_ref, gap_ref, dft_ref, inv_high_ref, inv_low_ref, angle_ref, x_ref, g_ref,
    res_ref, rates_ref, state_ref, weighted_ref,
    y_ref, gs_ref, gres_ref, grate_ref,
    inbox, outbox, landed, y_held, gs_held, sum_held, moment_held, rate_held,
    sumbox, ratebox, rowbox, rowrate, gathered, *sems,
):
    step = pl.program_id(0)
    sub = rate_ref.shape[0]
    length = x_ref.shape[0]
    channels = res_ref.shape[1]
    span = sub * LANES
    me = lax.axis_index("seq")
    mine = lax.axis_index("batch")
    width = channels // n
    others = [lax.rem(me + k, n) for k in range(1, n)]
    beside = [lax.rem(mine + k, rows) for k in range(1, rows)]
    pairs = [(sems[2 * i], sems[2 * i + 1]) for i in range(7)]

    def lanes(index):
        return pl.ds(pl.multiple_of(index * width, 128), width)

    def first():
        return [
            remote(state_ref.at[:, :, lanes(p)], inbox.at[me], pairs[0], k, "seq", p)
            for k, p in enumerate(others)
        ]

    def second():
        return [
            remote(outbox.at[p], landed.at[:, :, lanes(me)], pairs[1], k, "seq", p)
            for k, p in enumerate(others)
        ]

    def third():
        return [
            remote(sum_held.at[:, lanes(p)], sumbox.at[me], pairs[2], k, "seq", p)
            for k, p in enumerate(others)
        ] + [
            remote(rate_held, ratebox.at[me], pairs[3], k, "seq", p) for k, p in enumerate(others)
        ]

    def fourth():
        return [
            remote(rowbox.at[mine], rowbox.at[mine], pairs[4], k, "batch", p)
            for k, p in enumerate(beside)
        ] + [
            remote(rowrate.at[mine], rowrate.at[mine], pairs[5], k, "batch", p)
            for k, p in enumerate(beside)
        ]

    def fifth():
        return [
            remote(gathered.at[:, lanes(me)], gathered.at[:, lanes(me)], pairs[6], k, "seq", p)
            for k, p in enumerate(others)
        ]

    @pl.when(step == 0)
    def _():
        barrier = pltpu.get_barrier_semaphore()
        for p in others:
            pl.semaphore_signal(barrier, inc=1, device_id={"seq": p}, device_id_type=MESH)
        for p in beside:
            pl.semaphore_signal(barrier, inc=1, device_id={"batch": p}, device_id_type=MESH)
        pl.semaphore_wait(barrier, len(others) + len(beside))
        for copy in first():
            copy.start()

    @pl.when(step == steps // 2)
    def _():
        for copy in first():
            copy.wait_recv()
        inbox[me] = state_ref[:, :, lanes(me)]
        whole = jnp.exp(-rates_ref[:, lanes(me)] * float(length))
        carry = jnp.zeros_like(whole)
        adjoint = jnp.zeros_like(whole)
        for i in range(n):
            outbox[i, 0] = carry
            carry = inbox[i, 0] + whole * carry
            last = n - 1 - i
            outbox[last, 1] = adjoint
            adjoint = inbox[last, 1] + whole * adjoint
        for copy in second():
            copy.start()
        landed[:, :, lanes(me)] = outbox[me]

    @pl.when(step < steps)
    def _():
        for j in range(sub):
            here = slice(j * LANES, (j + 1) * LANES)
            at = pl.ds(pl.multiple_of(step * span + j * LANES, 128), LANES)
            y, gs, sums, moments = nega_block(
                modes, group, pole_ref[j], gap_ref[j], dft_ref[...], inv_high_ref[...],
                inv_low_ref[...], angle_ref[...], x_ref[:, here], g_ref[:, here], res_ref[:, at],
            )
            y_held[:, at] = y
            gs_held[:, at] = gs
            sum_held[:, at] = sums
            moment_held[:, at] = moments

    @pl.when(step == steps)
    def _():
        for copy in second():
            copy.wait_recv()
        per = LANES // group
        many = 128 // per
        row_id = lax.broadcasted_iota(jnp.int32, (LANES, 128), 0) // group
        col_id = lax.broadcasted_iota(jnp.int32, (LANES, 128), 1)

        def lap(c, nothing):
            added = jnp.zeros((2 * modes, 128), F32)
            for j in range(many):
                at = pl.ds(pl.multiple_of((c * many + j) * LANES, 128), LANES)
                rate = rates_ref[:, at]
                pole = jnp.exp(-rate)
                whole = jnp.exp(-rate * float(length))
                fold = 1.0 / (1.0 + whole)
                s_x, s_g = state_ref[0, :, at], state_ref[1, :, at]
                carry, adjoint = landed[0, :, at], landed[1, :, at]
                turned_x, turned_g = s_x * fold, s_g * fold
                carry_all, adjoint_all = carry + turned_x, adjoint + turned_g
                res = res_ref[:, at]
                sum_held[:, at] = sum_held[:, at] + carry_all * pole * s_g
                moments = (
                    moment_held[:, at]
                    + pole * (carry_all * weighted_ref[1, :, at] + adjoint_all * weighted_ref[0, :, at])
                    + float(length) * pole * whole * (carry * adjoint - turned_x * turned_g)
                )
                landed[0, :, at] = res * carry_all
                landed[1, :, at] = res * adjoint_all
                pick = jnp.where(row_id + j * per == col_id, 1.0, 0.0).astype(BF16)
                added += mul(jnp.concatenate(split(-rate * res * moments), 0), pick)
            rate_held[:, pl.ds(pl.multiple_of(c * 128, 128), 128)] = added[:modes] + added[modes:]
            return nothing

        lax.fori_loop(0, channels // (LANES * many), lap, 0)
        for copy in third():
            copy.start()
        sumbox[me] = sum_held[:, lanes(me)]
        ratebox[me] = rate_held[...]

    @pl.when(step >= steps)
    def _():
        for j in range(sub):
            here = slice(j * LANES, (j + 1) * LANES)
            at = pl.ds(pl.multiple_of((step - steps) * span + j * LANES, 128), LANES)
            rate = rate_ref[j]
            when = lax.broadcasted_iota(jnp.int32, (length, rate.shape[1]), 0).astype(F32)
            rising = jnp.exp(-rate * (when + 1.0))
            falling = jnp.exp(-rate * (length - when))
            y = y_held[:, at] + carry_block(group, rising, landed[0, :, at])
            y_ref[:, here] = y.astype(BF16)
            gs = gs_held[:, at] + carry_block(group, falling, landed[1, :, at])
            gs_ref[:, here] = gs.astype(BF16)

    @pl.when(step == 2 * steps - 1)
    def _():
        for copy in third():
            copy.wait_recv()
        part, rate_part = sumbox[0], ratebox[0]
        for i in range(1, n):
            part = part + sumbox[i]
            rate_part = rate_part + ratebox[i]
        rowbox[mine] = part
        rowrate[mine] = rate_part
        for copy in fourth():
            copy.start()
        for copy in fourth():
            copy.wait_recv()
        part, rate_part = rowbox[0], rowrate[0]
        for i in range(1, rows):
            part = part + rowbox[i]
            rate_part = rate_part + rowrate[i]
        gathered[:, lanes(me)] = part * norm
        for copy in fifth():
            copy.start()
        grate_ref[...] = rate_part * norm
        for copy in fifth():
            copy.wait_recv()
        gres_ref[...] = gathered[...]
        for copy in first() + second() + third() + fourth() + fifth():
            copy.wait_send()


def constants(length):
    half = length // 2
    omega = np.pi * (2.0 * np.arange(half) + 1.0) / length
    at = np.arange(length)
    forward = np.concatenate([np.cos(np.outer(omega, at)), -np.sin(np.outer(omega, at))], axis=0)
    lanes = np.ones((1, 128))
    angle = np.stack(
        [2.0 * np.sin(omega / 2.0)[:, None] ** 2 * lanes, np.sin(omega)[:, None] * lanes]
    )
    return forward.astype(np.float32), (forward.T / half).astype(np.float32), angle.astype(np.float32)


def local(mesh_shape, signal, out_grad, residues, log_rates):
    batch_rows, length, channels = signal.shape
    modes, groups = log_rates.shape
    group = channels // groups
    blocks = channels // LANES
    gm = LANES // group * modes
    norm = 1.0 / (batch_rows * mesh_shape["batch"] * length * mesh_shape["seq"])
    decay = jnp.exp(log_rates)
    flat = decay.T.reshape(blocks, 1, gm)
    pole = jnp.exp(-flat)
    gap = -jnp.expm1(-flat)
    lane_rate = jnp.repeat(decay, group, axis=1)
    forward, inverse, angle = constants(length)
    dft_high = jnp.asarray(forward).astype(BF16)
    dft = jnp.concatenate(
        [dft_high, (jnp.asarray(forward) - dft_high.astype(F32)).astype(BF16)], axis=1
    )
    inv_high, inv_low = split(jnp.asarray(inverse))
    angle = jnp.asarray(angle)
    peers, rows = mesh_shape["seq"], mesh_shape["batch"]
    width = channels // peers

    def specs(sub):
        return (
            pl.BlockSpec((sub, 1, gm), lambda b: (b, 0, 0)),
            pl.BlockSpec((length, sub * LANES), lambda b: (0, b)),
            pl.BlockSpec((modes, sub * LANES), lambda b: (0, b)),
            pl.BlockSpec((2, modes, sub * LANES), lambda b: (0, 0, b)),
        )

    def fixed(shape):
        return pl.BlockSpec(shape, lambda b: (0,) * len(shape))

    def dma(count):
        return pltpu.SemaphoreType.DMA((max(count, 1),))

    pair = jax.ShapeDtypeStruct((2, modes, channels), F32)
    mixed, grads, res_sum, rate_sum = [], [], 0.0, 0.0
    for row in range(batch_rows):
        x, g = signal[row], out_grad[row]
        row_spec, data_spec, lane_spec, pair_spec = specs(STATE_SUB)
        state, weighted = pl.pallas_call(
            functools.partial(states_kernel, modes, group),
            grid=(blocks // STATE_SUB,),
            in_specs=[row_spec, data_spec, data_spec],
            out_specs=[pair_spec, pair_spec],
            out_shape=[pair, pair],
        )(flat, x, g)
        steps = blocks // MAIN_SUB
        wide = MAIN_SUB * LANES
        y, gs, part, rates = pl.pallas_call(
            functools.partial(whole_kernel, peers, rows, norm, modes, group, steps),
            grid=(2 * steps,),
            in_specs=[pl.BlockSpec((MAIN_SUB, 1, gm), lambda b: (b % steps, 0, 0))] * 3
            + [fixed(v.shape) for v in (dft, inv_high, inv_low, angle)]
            + [pl.BlockSpec((length, wide), lambda b: (0, jnp.minimum(b, steps - 1)))] * 2
            + [fixed(residues.shape), fixed(lane_rate.shape), fixed(pair.shape), fixed(pair.shape)],
            out_specs=[pl.BlockSpec((length, wide), lambda b: (0, jnp.maximum(b - steps, 0)))] * 2
            + [fixed((modes, channels)), fixed((modes, groups))],
            out_shape=[
                jax.ShapeDtypeStruct((length, channels), BF16),
                jax.ShapeDtypeStruct((length, channels), BF16),
                jax.ShapeDtypeStruct((modes, channels), F32),
                jax.ShapeDtypeStruct((modes, groups), F32),
            ],
            scratch_shapes=[
                pltpu.VMEM((peers, 2, modes, width), F32),
                pltpu.VMEM((peers, 2, modes, width), F32),
                pltpu.VMEM((2, modes, channels), F32),
                pltpu.VMEM((length, channels), F32),
                pltpu.VMEM((length, channels), F32),
                pltpu.VMEM((modes, channels), F32),
                pltpu.VMEM((modes, channels), F32),
                pltpu.VMEM((modes, groups), F32),
                pltpu.VMEM((peers, modes, width), F32),
                pltpu.VMEM((peers, modes, groups), F32),
                pltpu.VMEM((rows, modes, width), F32),
                pltpu.VMEM((rows, modes, groups), F32),
                pltpu.VMEM((modes, channels), F32),
            ]
            + [dma(peers - 1)] * 8 + [dma(rows - 1)] * 4 + [dma(peers - 1)] * 2,
            compiler_params=pltpu.CompilerParams(collective_id=0, has_side_effects=True),
        )(flat, pole, gap, dft, inv_high, inv_low, angle, x, g, residues, lane_rate, state, weighted)
        mixed.append(y)
        grads.append(gs)
        res_sum = res_sum + part if row else part
        rate_sum = rate_sum + rates if row else rates
    return jnp.stack(mixed), jnp.stack(grads), res_sum, rate_sum


def solution(mesh):
    placed = (P("batch", "seq", None), P("batch", "seq", None), P(), P())
    return jax.shard_map(
        functools.partial(local, dict(mesh.shape)),
        mesh=mesh,
        in_specs=placed,
        out_specs=placed,
        check_vma=False,
    )
```

time: 278 us -> 76.1 us (0.27)
  waiting for transfers between devices: 158 us -> 0 us
  blocking collectives: 38.9 us -> 0 us
  Pallas kernels: 50.4 us -> 64.2 us
  between operations: 14.1 us -> 0.68 us
  other arithmetic: 7.25 us -> 0.62 us
  local copies, waits for them, and re-layouts: 5.58 us -> 9.75 us
    psum x1 -> x0, waiting for transfers between devices: 85.3 us -> none  [local(): lax.psum((res_sum * norm, rate_sum * norm), ('seq', 'batch'))]
    all_gather x1 -> x0, waiting for transfers between devices: 72.7 us -> none  [local(): every = lax.all_gather(state, 'seq')]
    psum x1 -> x0, blocking collectives: 38.9 us -> none  [local(): lax.psum((res_sum * norm, rate_sum * norm), ('seq', 'batch'))]
    pallas_call x1, Pallas kernels: 29.9 us -> 56.5 us  [local(): pl.pallas_call(functools.partial(whole_kernel, peers, rows, norm, modes,...]
    pallas_call x1, Pallas kernels: 20.5 us -> 7.65 us  [local(): pl.pallas_call(functools.partial(states_kernel, modes, group), grid=(bloc...]
    unnamed x5 -> x12, local copies, waits for them, and re-layouts: 1.68 us -> 5.89 us
    reduce_sum x1 -> x0, other arithmetic: 3.16 us -> none  [local(): jnp.sum(from_left * every[:, 0], axis=0)]
  transfers between devices with their start and end apart: 2 -> 0, of which waited for: 2 -> 0; matrix products, arithmetic and copies ran while one was open for 1% -> 0% of each run, Pallas kernels for 0% -> 0%
where the time goes in v3:
time: 76.1 us; the launch traced here: 75.2 us
  Pallas kernels  64.2 us (84%)
  local copies, waits for them, and re-layouts  9.75 us (13%)
    pallas_call x1, Pallas kernels, local(): pl.pallas_call(functools.partial(whole_kernel, peers, rows, norm, modes,...  56.5 us
    pallas_call x1, Pallas kernels, local(): pl.pallas_call(functools.partial(states_kernel, modes, group), grid=(bloc...  7.65 us
    unnamed x12, local copies, waits for them, and re-layouts  5.89 us
    reshape x1, local copies, waits for them, and re-layouts, local(): lane_rate = jnp.repeat(decay, group, axis=1)  2.26 us

profile of v3, /device:TPU:0, one launch (start us, length us, event | category | flops | bytes accessed | tf_op | source)
XLA Modules:
  0.0 75.2 jit_solution(15143898037353049469)
XLA Ops:
  0.6 0.7 fusion
  1.4 0.1 copy.16
  1.5 0.2 reshape.42
  1.6 0.0 copy-start.1
  1.7 0.6 exponential-minus-one_negate_fusion
  2.3 0.0 copy-done.1
  2.3 7.6 %shard_map.102 = (f32[2,8,8192]{2,1,0:T(8,128)}, f32[2,8,8192]{2,1,0:T(8,128)}) custom-call(f32[32,1,128]{2,1,0:T(1,128)} %bitcast.17, bf16[128,8192]{1,0:T(8,128)(2,1)} %bitcast.11, bf16[128,8192]{1,0:T(8,128)(2,1)} %bitcast.13), custom_call_target="tpu_custom_call" | custom-call | tf_op jit(solution)/shard_map/pallas_call | solution.py:361
  9.9 0.6 broadcast_in_dim.3
  10.5 2.3 %reshape.43.rates_ref = f32[8,8192]{1,0:T(8,128)} reshape(f32[8,512,16]{2,1,0:T(8,128)S(1)} %broadcast_in_dim.3) | data formatting | bytes 524288 | tf_op jit(solution)/shard_map/reshape | solution.py:331
  12.8 56.5 %shard_map.103 = (bf16[128,8192]{1,0:T(8,128)(2,1)}, bf16[128,8192]{1,0:T(8,128)(2,1)}, f32[8,8192]{1,0:T(8,128)}, f32[8,512]{1,0:T(8,128)}) custom-call(f32[32,1,128]{2,1,0:T(1,128)} %bitcast.18, f32[32,1,128]{2,1,0:T(1,128)} %bitcast.20, f32[32,1,128]{2,1,0:T(1,128)} %bitcast.19, bf16[128,256]{1,0:T(8,128)(2,1)} %constant.15.dft_ref, ...), custom_call_target="tpu_custom_call" | custom-call | tf_op jit(solution)/shard_map/pallas_call | solution.py:370
  69.3 0.0 copy-start
  69.3 3.2 %copy.25 = bf16[1,128,8192]{2,1,0:T(8,128)(2,1)} copy(bf16[1,128,8192]{2,1,0:T(8,128)(2,1)} %bitcast.16) | data formatting | bytes 4194304
  72.6 0.0 copy-done
  72.6 0.0 copy-start.2
  72.6 0.0 copy-start.3
  72.6 1.3 %copy.26 = bf16[1,128,8192]{2,1,0:T(8,128)(2,1)} copy(bf16[1,128,8192]{2,1,0:T(8,128)(2,1)S(1)} %bitcast.15) | data formatting | bytes 4194304
  73.9 0.0 copy-done.2
  73.9 0.7 copy.27
  74.6 0.0 copy-done.3
  74.6 0.6 copy.28
  (1 shorter events, 0.0 us)
Async XLA Ops:
  1.6 0.6 copy-start.1
  69.3 3.3 %copy-start = (bf16[128,8192]{1,0:T(8,128)(2,1)S(1)}, bf16[128,8192]{1,0:T(8,128)(2,1)}, u32[]{:S(2)}) copy-start(bf16[128,8192]{1,0:T(8,128)(2,1)} %get-tuple-element.13) | copy-start | bytes 6291460
  72.6 1.3 %copy-start.2 = (f32[8,8192]{1,0:T(8,128)S(1)}, f32[8,8192]{1,0:T(8,128)}, u32[]{:S(2)}) copy-start(f32[8,8192]{1,0:T(8,128)} %get-tuple-element.28) | copy-start | bytes 786436
  72.6 2.0 %copy-start.3 = (f32[8,512]{1,0:T(8,128)S(1)}, f32[8,512]{1,0:T(8,128)}, u32[]{:S(2)}) copy-start(f32[8,512]{1,0:T(8,128)} %get-tuple-element.29) | copy-start | bytes 49156

commit v4 on v3

--- a/solution.py
+++ b/solution.py
@@ -13,7 +13,7 @@
 BF16 = jnp.bfloat16
 MESH = pl.DeviceIdType.MESH
 STATE_SUB = 4
-MAIN_SUB = 2
+MAIN_SUB = 4
 
 
 def split(value):

time: 76.1 us -> 75.4 us (level)
  no operation moved by 1% of the time
where the time goes in v4:
time: 75.4 us; the launch traced here: 74.7 us
  Pallas kernels  63.7 us (84%)
  local copies, waits for them, and re-layouts  9.75 us (13%)
    pallas_call x1, Pallas kernels, local(): pl.pallas_call(functools.partial(whole_kernel, peers, rows, norm, modes,...  56 us
    pallas_call x1, Pallas kernels, local(): pl.pallas_call(functools.partial(states_kernel, modes, group), grid=(bloc...  7.65 us
    unnamed x12, local copies, waits for them, and re-layouts  5.89 us
    reshape x1, local copies, waits for them, and re-layouts, local(): lane_rate = jnp.repeat(decay, group, axis=1)  2.26 us

profile of v4, /device:TPU:0, one launch (start us, length us, event | category | flops | bytes accessed | tf_op | source)
XLA Modules:
  0.0 74.7 jit_solution(10809885341538911630)
XLA Ops:
  0.6 0.7 fusion
  1.4 0.1 copy.16
  1.5 0.2 reshape.42
  1.6 0.0 copy-start.1
  1.7 0.6 exponential-minus-one_negate_fusion
  2.3 0.0 copy-done.1
  2.3 7.6 %shard_map.102 = (f32[2,8,8192]{2,1,0:T(8,128)}, f32[2,8,8192]{2,1,0:T(8,128)}) custom-call(f32[32,1,128]{2,1,0:T(1,128)} %bitcast.17, bf16[128,8192]{1,0:T(8,128)(2,1)} %bitcast.11, bf16[128,8192]{1,0:T(8,128)(2,1)} %bitcast.13), custom_call_target="tpu_custom_call" | custom-call | tf_op jit(solution)/shard_map/pallas_call | solution.py:361
  9.9 0.6 broadcast_in_dim.3
  10.5 2.3 %reshape.43.rates_ref = f32[8,8192]{1,0:T(8,128)} reshape(f32[8,512,16]{2,1,0:T(8,128)S(1)} %broadcast_in_dim.3) | data formatting | bytes 524288 | tf_op jit(solution)/shard_map/reshape | solution.py:331
  12.8 56.0 %shard_map.103 = (bf16[128,8192]{1,0:T(8,128)(2,1)}, bf16[128,8192]{1,0:T(8,128)(2,1)}, f32[8,8192]{1,0:T(8,128)}, f32[8,512]{1,0:T(8,128)}) custom-call(f32[32,1,128]{2,1,0:T(1,128)} %bitcast.18, f32[32,1,128]{2,1,0:T(1,128)} %bitcast.20, f32[32,1,128]{2,1,0:T(1,128)} %bitcast.19, bf16[128,256]{1,0:T(8,128)(2,1)} %constant.15.dft_ref, ...), custom_call_target="tpu_custom_call" | custom-call | tf_op jit(solution)/shard_map/pallas_call | solution.py:370
  68.8 0.0 copy-start
  68.8 3.2 %copy.25 = bf16[1,128,8192]{2,1,0:T(8,128)(2,1)} copy(bf16[1,128,8192]{2,1,0:T(8,128)(2,1)} %bitcast.16) | data formatting | bytes 4194304
  72.1 0.0 copy-done
  72.1 0.0 copy-start.2
  72.1 0.0 copy-start.3
  72.1 1.3 %copy.26 = bf16[1,128,8192]{2,1,0:T(8,128)(2,1)} copy(bf16[1,128,8192]{2,1,0:T(8,128)(2,1)S(1)} %bitcast.15) | data formatting | bytes 4194304
  73.4 0.0 copy-done.2
  73.4 0.7 copy.27
  74.1 0.0 copy-done.3
  74.1 0.6 copy.28
  (1 shorter events, 0.0 us)
Async XLA Ops:
  1.6 0.6 copy-start.1
  68.8 3.3 %copy-start = (bf16[128,8192]{1,0:T(8,128)(2,1)S(1)}, bf16[128,8192]{1,0:T(8,128)(2,1)}, u32[]{:S(2)}) copy-start(bf16[128,8192]{1,0:T(8,128)(2,1)} %get-tuple-element.13) | copy-start | bytes 6291460
  72.1 1.3 %copy-start.2 = (f32[8,8192]{1,0:T(8,128)S(1)}, f32[8,8192]{1,0:T(8,128)}, u32[]{:S(2)}) copy-start(f32[8,8192]{1,0:T(8,128)} %get-tuple-element.28) | copy-start | bytes 786436
  72.1 2.0 %copy-start.3 = (f32[8,512]{1,0:T(8,128)S(1)}, f32[8,512]{1,0:T(8,128)}, u32[]{:S(2)}) copy-start(f32[8,512]{1,0:T(8,128)} %get-tuple-element.29) | copy-start | bytes 49156
